TPU v7x, 32 devices: a whole 2x2x4 slice. The times are simulated.
32 devices in a mesh: row: 8 (over y, x, core), col: 4 (over z).
Axes of the slice: x: 2, y: 2, z: 4, core: 2. Of those that a mesh axis runs over, the one named last changes fastest.
Arguments:
- block_values: bfloat16 [8, 4, 64, 256, 256], P('row', 'col'), may hold values from -0.1875 to 0.1875
- block_rows: int32 [8, 4, 64], P('row', 'col'), may hold values from 0 to 63
- block_cols: int32 [8, 4, 64], P('row', 'col'), may hold values from 0 to 255
- live_count: int32 [8, 4], P('row', 'col'), may hold values from 16 to 64, as said below
- objective: float32 [262144], P('col'), may hold values from -6 to 6
- upper_bound: float32 [262144], P('col'), may hold values from 0.5 to 2
- demand: float32 [131072], P('row'), may hold values from -6 to 6
- primal_start: float32 [262144], P('col'), may hold values from 0 to 0.5
- dual_start: float32 [131072], P('row'), may hold values from 0 to 0.5
- restart_at: int32 [8], replicated, may hold values 0 or 1
Outputs:
- primal_final: float32 [262144], P('col')
- dual_final: float32 [131072], P('row')
Inputs may be any that keep to these rules, and one draw needn't show every extreme that they name: `live_count`: each device's count of used slots; some device uses all 64.
All inputs are finite; a program needn't handle non-finite values.
Results may differ from a plain program's by a relative error of at most 0.0018.
Values may be sent and summed in bfloat16 or wider, within the bound.
A program may use at most 64 MiB of HBM per device.

v0:
```python
import jax
import jax.numpy as jnp
from jax import lax
from jax.sharding import PartitionSpec as P

ITERS = 8


step_scale = 0.3
epsilon = 1e-06


def shards(
    block_values,
    block_rows,
    block_cols,
    live_count,
    objective,
    upper_bound,
    demand,
    primal_start,
    dual_start,
    restart_at,
):
    slot_values = block_values[0, 0]
    rows_index = block_rows[0, 0]
    cols_index = block_cols[0, 0]
    used_slots = live_count[0, 0]
    slots = slot_values.shape[0]
    block_size = slot_values.shape[1]
    row_blocks = demand.shape[0] // block_size
    col_blocks = objective.shape[0] // block_size
    row_count = lax.axis_size("row")
    col_count = lax.axis_size("col")
    row_rank = lax.axis_index("row")
    col_rank = lax.axis_index("col")
    total_cols = objective.shape[0] * col_count
    total_rows = demand.shape[0] * row_count
    share_len = objective.shape[0] // row_count
    dual_len = demand.shape[0] // col_count
    live_slot = jnp.arange(slots, dtype=jnp.int32) < used_slots
    row_onehot = (
        (rows_index[:, None] == jnp.arange(row_blocks, dtype=jnp.int32)[None, :])
        & live_slot[:, None]
    ).astype(jnp.float32)
    col_onehot = (
        (cols_index[:, None] == jnp.arange(col_blocks, dtype=jnp.int32)[None, :])
        & live_slot[:, None]
    ).astype(jnp.float32)
    x = primal_start
    y = dual_start
    anchor_x = x
    anchor_y = y
    sum_x = jnp.zeros_like(x)
    sum_y = jnp.zeros_like(y)
    taken = jnp.zeros((), jnp.float32)
    omega = jnp.ones((), jnp.float32)
    for k in range(ITERS):
        step_primal = step_scale / omega
        step_dual = step_scale * omega
        y_low = y.astype(jnp.bfloat16)
        dual_pieces = y_low.reshape(row_blocks, block_size)[rows_index]
        dual_products = jnp.einsum(
            "tij,ti->tj", slot_values, dual_pieces, preferred_element_type=jnp.float32
        )
        dual_image = lax.psum(
            jnp.einsum(
                "tc,tj->cj", col_onehot, dual_products, precision=lax.Precision.HIGHEST
            ).reshape(-1),
            "row",
        )
        x_next = jnp.minimum(
            jnp.maximum(x - step_primal * (objective - dual_image), 0.0), upper_bound
        )
        extrap_low = (2.0 * x_next - x).astype(jnp.bfloat16)
        pieces = extrap_low.reshape(col_blocks, block_size)[cols_index]
        products = jnp.einsum("tij,tj->ti", slot_values, pieces, preferred_element_type=jnp.float32)
        primal_image = lax.psum(
            jnp.einsum("tr,ti->ri", row_onehot, products, precision=lax.Precision.HIGHEST).reshape(
                -1
            ),
            "col",
        )
        y_next = jnp.maximum(y + step_dual * (demand - primal_image), 0.0)
        x = x_next
        y = y_next
        sum_x = sum_x + x
        sum_y = sum_y + y
        taken = taken + 1.0
        if k <= ITERS - 3:
            is_restart = restart_at[k] == 1
            mean_x = sum_x / taken
            mean_y = sum_y / taken
            gap_x = lax.dynamic_slice_in_dim(mean_x - anchor_x, row_rank * share_len, share_len)
            gap_y = lax.dynamic_slice_in_dim(mean_y - anchor_y, col_rank * dual_len, dual_len)
            square_x = lax.psum(jnp.sum(gap_x * gap_x), ("row", "col"))
            square_y = lax.psum(jnp.sum(gap_y * gap_y), ("row", "col"))
            drift_x = square_x / total_cols + epsilon
            drift_y = square_y / total_rows + epsilon
            omega_next = jnp.sqrt(omega) * (drift_x / drift_y) ** 0.25
            x = jnp.where(is_restart, mean_x, x)
            y = jnp.where(is_restart, mean_y, y)
            anchor_x = jnp.where(is_restart, mean_x, anchor_x)
            anchor_y = jnp.where(is_restart, mean_y, anchor_y)
            sum_x = jnp.where(is_restart, jnp.zeros_like(sum_x), sum_x)
            sum_y = jnp.where(is_restart, jnp.zeros_like(sum_y), sum_y)
            taken = jnp.where(is_restart, jnp.zeros_like(taken), taken)
            omega = jnp.where(is_restart, omega_next, omega)
    return (x, y)


def solution(mesh):
    placed = (
        P("row", "col", None, None, None),
        P("row", "col", None),
        P("row", "col", None),
        P("row", "col"),
        P("col"),
        P("col"),
        P("row"),
        P("col"),
        P("row"),
        P(),
    )
    return jax.shard_map(
        shards, mesh=mesh, in_specs=placed, out_specs=(P("col"), P("row")), check_vma=False
    )
```

profile of v0, /device:TPU:0, one launch (start us, length us, event | category | flops | bytes accessed | tf_op | source)
XLA Modules:
  0.0 848.5 jit_solution(4290460746907200810)
XLA Ops:
  16.1 56.7 %all-reduce.23.cloned.1.call-done = f32[65536]{0:T(1024)} async-done(((f32[65536]{0:T(1024)}), f32[65536]{0:T(1024)}) %all-reduce.23.cloned.1.call-update) | async-done | bytes 262160 | tf_op jit(solution)/shard_map/psum | solution.py:66
  74.6 5.6 fusion.28
  81.3 33.8 %all-reduce.25.cloned.1.call-done = f32[16384]{0:T(1024)} async-done(((f32[16384]{0:T(1024)}), f32[16384]{0:T(1024)}) %all-reduce.25.cloned.1.call-update) | async-done | bytes 65552 | tf_op jit(solution)/shard_map/psum | solution.py:78
  125.9 40.4 %all-reduce.5 = (f32[]{:T(128)}, f32[]{:T(128)}) all-reduce(f32[]{:T(128)} %fusion.98, f32[]{:T(128)} %fusion.138), channel_id=1, replica_groups=mesh['row'=8,'col'=4] {'row','col'}, use_global_device_ids=true, to_apply=%region_2.0 | all-reduce | flops 2 | bytes 16 | tf_op jit(solution)/shard_map/psum | solution.py:96
  167.7 8.6 %all-reduce.27.cloned.1.call-done = f32[65536]{0:T(1024)} async-done(((f32[65536]{0:T(1024)}), f32[65536]{0:T(1024)}) %all-reduce.27.cloned.1.call-update) | async-done | bytes 262160 | tf_op jit(solution)/shard_map/psum | solution.py:66
  178.1 5.6 fusion.24
  184.8 33.8 %all-reduce.29.cloned.1.call-done = f32[16384]{0:T(1024)} async-done(((f32[16384]{0:T(1024)}), f32[16384]{0:T(1024)}) %all-reduce.29.cloned.1.call-update) | async-done | bytes 65552 | tf_op jit(solution)/shard_map/psum | solution.py:78
  227.5 40.3 %all-reduce.4 = (f32[]{:T(128)}, f32[]{:T(128)}) all-reduce(f32[]{:T(128)} %fusion.96, f32[]{:T(128)} %fusion.136), channel_id=1, replica_groups=mesh['row'=8,'col'=4] {'row','col'}, use_global_device_ids=true, to_apply=%region_8.9 | all-reduce | flops 2 | bytes 16 | tf_op jit(solution)/shard_map/psum | solution.py:96
  269.3 10.5 %all-reduce.31.cloned.1.call-done = f32[65536]{0:T(1024)} async-done(((f32[65536]{0:T(1024)}), f32[65536]{0:T(1024)}) %all-reduce.31.cloned.1.call-update) | async-done | bytes 262160 | tf_op jit(solution)/shard_map/psum | solution.py:66
  289.3 32.9 %all-reduce.33.cloned.1.call-done = f32[16384]{0:T(1024)} async-done(((f32[16384]{0:T(1024)}), f32[16384]{0:T(1024)}) %all-reduce.33.cloned.1.call-update) | async-done | bytes 65552 | tf_op jit(solution)/shard_map/psum | solution.py:78
  331.5 40.3 %all-reduce.3 = (f32[]{:T(128)}, f32[]{:T(128)}) all-reduce(f32[]{:T(128)} %fusion.94, f32[]{:T(128)} %fusion.134), channel_id=1, replica_groups=mesh['row'=8,'col'=4] {'row','col'}, use_global_device_ids=true, to_apply=%region_14.15 | all-reduce | flops 2 | bytes 16 | tf_op jit(solution)/shard_map/psum | solution.py:96
  373.1 10.3 %all-reduce.35.cloned.1.call-done = f32[65536]{0:T(1024)} async-done(((f32[65536]{0:T(1024)}), f32[65536]{0:T(1024)}) %all-reduce.35.cloned.1.call-update) | async-done | bytes 262160 | tf_op jit(solution)/shard_map/psum | solution.py:66
  391.9 33.8 %all-reduce.37.cloned.1.call-done = f32[16384]{0:T(1024)} async-done(((f32[16384]{0:T(1024)}), f32[16384]{0:T(1024)}) %all-reduce.37.cloned.1.call-update) | async-done | bytes 65552 | tf_op jit(solution)/shard_map/psum | solution.py:78
  434.5 40.3 %all-reduce.2 = (f32[]{:T(128)}, f32[]{:T(128)}) all-reduce(f32[]{:T(128)} %fusion.92, f32[]{:T(128)} %fusion.132), channel_id=1, replica_groups=mesh['row'=8,'col'=4] {'row','col'}, use_global_device_ids=true, to_apply=%region_20.21 | all-reduce | flops 2 | bytes 16 | tf_op jit(solution)/shard_map/psum | solution.py:96
  476.1 10.8 %all-reduce.39.cloned.1.call-done = f32[65536]{0:T(1024)} async-done(((f32[65536]{0:T(1024)}), f32[65536]{0:T(1024)}) %all-reduce.39.cloned.1.call-update) | async-done | bytes 262160 | tf_op jit(solution)/shard_map/psum | solution.py:66
  496.2 33.2 %all-reduce.41.cloned.1.call-done = f32[16384]{0:T(1024)} async-done(((f32[16384]{0:T(1024)}), f32[16384]{0:T(1024)}) %all-reduce.41.cloned.1.call-update) | async-done | bytes 65552 | tf_op jit(solution)/shard_map/psum | solution.py:78
  538.1 40.3 %all-reduce.1 = (f32[]{:T(128)}, f32[]{:T(128)}) all-reduce(f32[]{:T(128)} %multiply_reduce_fusion, f32[]{:T(128)} %multiply_reduce_fusion.1), channel_id=1, replica_groups=mesh['row'=8,'col'=4] {'row','col'}, use_global_device_ids=true, to_apply=%region_26.27 | all-reduce | flops 2 | bytes 16 | tf_op jit(solution)/shard_map/psum | solution.py:96
  579.9 10.7 %all-reduce.43.cloned.1.call-done = f32[65536]{0:T(1024)} async-done(((f32[65536]{0:T(1024)}), f32[65536]{0:T(1024)}) %all-reduce.43.cloned.1.call-update) | async-done | bytes 262160 | tf_op jit(solution)/shard_map/psum | solution.py:66
  600.0 33.0 %all-reduce.45.cloned.1.call-done = f32[16384]{0:T(1024)} async-done(((f32[16384]{0:T(1024)}), f32[16384]{0:T(1024)}) %all-reduce.45.cloned.1.call-update) | async-done | bytes 65552 | tf_op jit(solution)/shard_map/psum | solution.py:78
  641.7 40.4 %all-reduce = (f32[]{:T(128)}, f32[]{:T(128)}) all-reduce(f32[]{:T(128)} %fusion.90, f32[]{:T(128)} %fusion.130), channel_id=1, replica_groups=mesh['row'=8,'col'=4] {'row','col'}, use_global_device_ids=true, to_apply=%region_32.33 | all-reduce | flops 2 | bytes 16 | tf_op jit(solution)/shard_map/psum | solution.py:96
  683.5 10.6 %all-reduce.47.cloned.1.call-done = f32[65536]{0:T(1024)} async-done(((f32[65536]{0:T(1024)}), f32[65536]{0:T(1024)}) %all-reduce.47.cloned.1.call-update) | async-done | bytes 262160 | tf_op jit(solution)/shard_map/psum | solution.py:66
  702.6 33.8 %all-reduce.49.cloned.1.call-done = f32[16384]{0:T(1024)} async-done(((f32[16384]{0:T(1024)}), f32[16384]{0:T(1024)}) %all-reduce.49.cloned.1.call-update) | async-done | bytes 65552 | tf_op jit(solution)/shard_map/psum | solution.py:78
  743.9 53.7 %all-reduce.51.cloned.1.call-done = f32[65536]{0:T(1024)} async-done(((f32[65536]{0:T(1024)}), f32[65536]{0:T(1024)}) %all-reduce.51.cloned.1.call-update) | async-done | bytes 262160 | tf_op jit(solution)/shard_map/psum | solution.py:66
  806.7 33.8 %all-reduce.53.cloned.1.call-done = f32[16384]{0:T(1024)} async-done(((f32[16384]{0:T(1024)}), f32[16384]{0:T(1024)}) %all-reduce.53.cloned.1.call-update) | async-done | bytes 65552 | tf_op jit(solution)/shard_map/psum | solution.py:78
  (168 shorter events, 127.7 us)
Async XLA Ops:
  7.2 7.6 copy-start.5
  7.2 65.6 %all-reduce.23.cloned.1.call-start = ((), (), s32[]{:S(2)}) async-start(), calls=%async_computation | async-start | bytes 524288 | tf_op jit(solution)/shard_map/psum | solution.py:66
  10.1 62.7 %copy-start = (f32[65536]{0:T(1024)S(1)}, f32[65536]{0:T(1024)}, u32[]{:S(2)}) copy-start(f32[65536]{0:T(1024)} %param.15) | copy-start | bytes 786436
  10.1 62.7 %copy-start.1 = (f32[65536]{0:T(1024)S(1)}, f32[65536]{0:T(1024)}, u32[]{:S(2)}) copy-start(f32[65536]{0:T(1024)} %param.14) | copy-start | bytes 786436
  10.1 62.7 %copy-start.3 = (f32[65536]{0:T(1024)S(1)}, f32[65536]{0:T(1024)}, u32[]{:S(2)}) copy-start(f32[65536]{0:T(1024)} %param.17) | copy-start | bytes 786436
  14.8 65.4 %copy-start.6 = (s32[1,1,64]{2,1,0:T(1,128)S(1)}, s32[1,1,64]{2,1,0:T(1,128)}, u32[]{:S(2)}) copy-start(s32[1,1,64]{2,1,0:T(1,128)} %param.11) | copy-start | bytes 772
  14.8 100.3 %copy-start.2 = (f32[16384]{0:T(1024)S(1)}, f32[16384]{0:T(1024)}, u32[]{:S(2)}) copy-start(f32[16384]{0:T(1024)} %param.16) | copy-start | bytes 196612
  14.8 100.3 %copy-start.4 = (f32[16384]{0:T(1024)S(1)}, f32[16384]{0:T(1024)}, u32[]{:S(2)}) copy-start(f32[16384]{0:T(1024)} %param.18) | copy-start | bytes 196612
  16.1 99.0 %all-reduce.25.cloned.1.call-start = ((), (), s32[]{:S(2)}) async-start(), calls=%async_computation.1 | async-start | bytes 131072 | tf_op jit(solution)/shard_map/psum | solution.py:78
  81.2 95.0 %all-reduce.27.cloned.1.call-start = ((), (), s32[]{:S(2)}) async-start(), calls=%async_computation.2 | async-start | bytes 524288 | tf_op jit(solution)/shard_map/psum | solution.py:66
  116.7 5.9 copy-start.7
  122.5 96.1 %all-reduce.29.cloned.1.call-start = ((), (), s32[]{:S(2)}) async-start(), calls=%async_computation.3 | async-start | bytes 131072 | tf_op jit(solution)/shard_map/psum | solution.py:78
  184.8 95.1 %all-reduce.31.cloned.1.call-start = ((), (), s32[]{:S(2)}) async-start(), calls=%async_computation.4 | async-start | bytes 524288 | tf_op jit(solution)/shard_map/psum | solution.py:66
  226.1 96.1 %all-reduce.33.cloned.1.call-start = ((), (), s32[]{:S(2)}) async-start(), calls=%async_computation.5 | async-start | bytes 131072 | tf_op jit(solution)/shard_map/psum | solution.py:78
  288.3 95.1 %all-reduce.35.cloned.1.call-start = ((), (), s32[]{:S(2)}) async-start(), calls=%async_computation.6 | async-start | bytes 524288 | tf_op jit(solution)/shard_map/psum | solution.py:66
  329.6 96.1 %all-reduce.37.cloned.1.call-start = ((), (), s32[]{:S(2)}) async-start(), calls=%async_computation.7 | async-start | bytes 131072 | tf_op jit(solution)/shard_map/psum | solution.py:78
  391.9 95.1 %all-reduce.39.cloned.1.call-start = ((), (), s32[]{:S(2)}) async-start(), calls=%async_computation.8 | async-start | bytes 524288 | tf_op jit(solution)/shard_map/psum | solution.py:66
  433.2 96.1 %all-reduce.41.cloned.1.call-start = ((), (), s32[]{:S(2)}) async-start(), calls=%async_computation.9 | async-start | bytes 131072 | tf_op jit(solution)/shard_map/psum | solution.py:78
  495.5 95.1 %all-reduce.43.cloned.1.call-start = ((), (), s32[]{:S(2)}) async-start(), calls=%async_computation.10 | async-start | bytes 524288 | tf_op jit(solution)/shard_map/psum | solution.py:66
  536.8 96.1 %all-reduce.45.cloned.1.call-start = ((), (), s32[]{:S(2)}) async-start(), calls=%async_computation.11 | async-start | bytes 131072 | tf_op jit(solution)/shard_map/psum | solution.py:78
  599.1 95.0 %all-reduce.47.cloned.1.call-start = ((), (), s32[]{:S(2)}) async-start(), calls=%async_computation.12 | async-start | bytes 524288 | tf_op jit(solution)/shard_map/psum | solution.py:66
  640.4 96.0 %all-reduce.49.cloned.1.call-start = ((), (), s32[]{:S(2)}) async-start(), calls=%async_computation.13 | async-start | bytes 131072 | tf_op jit(solution)/shard_map/psum | solution.py:78
  702.5 95.0 %all-reduce.51.cloned.1.call-start = ((), (), s32[]{:S(2)}) async-start(), calls=%async_computation.14 | async-start | bytes 524288 | tf_op jit(solution)/shard_map/psum | solution.py:66
  743.8 96.7 %all-reduce.53.cloned.1.call-start = ((), (), s32[]{:S(2)}) async-start(), calls=%async_computation.15 | async-start | bytes 131072 | tf_op jit(solution)/shard_map/psum | solution.py:78
Sparse Core Ops, SparseCore 0:
  16.2 56.5 all-reduce.22
  81.4 33.6 all-reduce.24
  122.7 53.5 all-reduce.26
  184.9 33.6 all-reduce.28
  226.2 53.5 all-reduce.30
  288.5 33.7 all-reduce.32
  329.8 53.5 all-reduce.34
  392.0 33.6 all-reduce.36
  433.3 53.6 all-reduce.38
  495.6 33.6 all-reduce.40
  536.9 53.6 all-reduce.42
  599.2 33.6 all-reduce.44
  640.5 53.5 all-reduce.46
  702.7 33.6 all-reduce.48
  743.9 53.5 all-reduce.50
  806.8 33.6 all-reduce.52
where the time goes:
time: 850 us; the launch traced here: 849 us
  waiting for transfers between devices  440 us (52%)
  blocking collectives  242 us (28%)
  matrix products  87.5 us (10%)
  between operations  27.6 us (3%)
  other arithmetic  25.7 us (3%)
  local copies, waits for them, and re-layouts  24.5 us (3%)
    psum x8, waiting for transfers between devices, shards(): lax.psum(jnp.einsum('tr,ti->ri', row_onehot, products, precision=lax.Prec...  268 us
    psum x6, blocking collectives, shards(): square_x = lax.psum(jnp.sum(gap_x * gap_x), ('row', 'col'))  242 us
    psum x8, waiting for transfers between devices, shards(): lax.psum(jnp.einsum('tc,tj->cj', col_onehot, dual_products, precision=lax...  172 us
    dot_general x8, matrix products, shards(): jnp.einsum('tij,tj->ti', slot_values, pieces, preferred_element_type=jnp....  45.1 us
    dot_general x8, matrix products, shards(): jnp.einsum('tij,ti->tj', slot_values, dual_pieces, preferred_element_type...  36.7 us
  transfers between devices with their start and end apart: 16, of which 16 were waited for; matrix products, arithmetic and copies ran while one was open for 1% of the time, Pallas kernels for 0%

commit v1 on v0

v1 whole, which is shorter than its diff:
```python
import functools

import jax
import jax.numpy as jnp
from jax import lax
from jax.experimental import pallas as pl
from jax.experimental.pallas import tpu as pltpu
from jax.sharding import PartitionSpec as P

ITERS = 8
GROUP = 16
CHUNKS = 2

step_scale = 0.3
epsilon = 1e-06

MESH = pl.DeviceIdType.MESH


def fold(v):
    rows, lanes = v.shape
    v = jnp.sum(v.reshape(rows // 8, 8, lanes), axis=0)
    out = v[:, 0:128]
    for i in range(1, lanes // 128):
        out = out + v[:, 128 * i : 128 * (i + 1)]
    return out


def kernel(
    n_row,
    n_col,
    slots,
    block,
    k_hbm,
    idx_ref,
    restart_ref,
    obj_ref,
    ub_ref,
    dem_ref,
    x0_ref,
    y0_ref,
    xo_ref,
    yo_ref,
    k_v,
    ridx,
    cidx,
    oh_d,
    oh_p,
    oh_c,
    oh_r,
    drecv,
    precv,
    dyr,
    dxr,
    obj_s,
    ub_s,
    dem_s,
    x_s,
    y_s,
    ax_s,
    ay_s,
    sx_s,
    sy_s,
    ksem,
    is_r,
    ir_r,
    is_c,
    ir_c,
    ds_sem,
    dr_sem,
    ps_sem,
    pr_sem,
    ys_sem,
    yr_sem,
    xs_sem,
    xr_sem,
):
    me_r = lax.axis_index("row")
    me_c = lax.axis_index("col")
    col_blocks = x_s.shape[0]
    row_blocks = y_s.shape[0]
    total_cols = float(col_blocks * block * n_col)
    total_rows = float(row_blocks * block * n_row)
    bf16, f32 = jnp.bfloat16, jnp.float32
    groups = slots // GROUP
    per_chunk = slots // CHUNKS

    kcopies = []
    for g in range(groups):
        part = pl.ds(g * GROUP * block, GROUP * block)
        c = pltpu.make_async_copy(k_hbm.at[part, :], k_v.at[part, :], ksem.at[g])
        c.start()
        kcopies.append(c)

    row_peers = [lax.rem(me_r + d, n_row) for d in range(n_row - 1, 0, -1)]
    col_peers = [lax.rem(me_c + d, n_col) for d in range(n_col - 1, 0, -1)]

    barrier = pltpu.get_barrier_semaphore()
    for p in row_peers:
        pl.semaphore_signal(barrier, inc=1, device_id={"row": p}, device_id_type=MESH)
    for p in col_peers:
        pl.semaphore_signal(barrier, inc=1, device_id={"col": p}, device_id_type=MESH)

    half = block // 2

    def widen(ref, n):
        return jnp.concatenate(
            [ref[pl.ds(0, n, stride=2), :], ref[pl.ds(1, n, stride=2), :]], axis=1
        )

    obj_s[...] = widen(obj_ref, col_blocks)
    ub_s[...] = widen(ub_ref, col_blocks)
    dem_s[...] = widen(dem_ref, row_blocks)
    x_first = widen(x0_ref, col_blocks)
    y_first = widen(y0_ref, row_blocks)
    x_s[...] = x_first
    ax_s[...] = x_first
    sx_s[...] = jnp.zeros_like(x_first)
    y_s[...] = y_first
    ay_s[...] = y_first
    sy_s[...] = jnp.zeros_like(y_first)
    dyr[0, me_r] = jnp.zeros((8, 128), f32)
    dyr[1, me_r] = jnp.zeros((8, 128), f32)
    for c in range(n_col):
        dxr[1, c] = jnp.zeros((8, 128), f32)

    own_cols = idx_ref[0:1, :]
    own_rows = idx_ref[1:2, :]
    oh = (own_cols == lax.broadcasted_iota(jnp.int32, (col_blocks, 128), 0)).astype(f32)
    oh_c[...] = jnp.transpose(oh)[:slots, :].astype(bf16)
    pad = -(-row_blocks // 128) * 128
    oh = (own_rows == lax.broadcasted_iota(jnp.int32, (pad, 128), 0)).astype(f32)
    oh_r[...] = jnp.transpose(oh)[:slots, :row_blocks].astype(bf16)

    pl.semaphore_wait(barrier, n_row + n_col - 2)

    def remote(src, dst, ssem, rsem, axis, peer):
        return pltpu.make_async_remote_copy(
            src_ref=src,
            dst_ref=dst,
            send_sem=ssem,
            recv_sem=rsem,
            device_id={axis: peer},
            device_id_type=MESH,
        )

    ridx[me_r] = idx_ref[...]
    cidx[me_c] = idx_ref[...]
    for p in row_peers:
        remote(idx_ref, ridx.at[me_r], is_r.at[p], ir_r.at[me_r], "row", p).start()
    for p in col_peers:
        remote(idx_ref, cidx.at[me_c], is_c.at[p], ir_c.at[me_c], "col", p).start()
    for p in row_peers:
        remote(idx_ref, ridx.at[p], is_r.at[p], ir_r.at[p], "row", p).wait()
    for p in col_peers:
        remote(idx_ref, cidx.at[p], is_c.at[p], ir_c.at[p], "col", p).wait()

    every = jnp.concatenate([ridx[r][0:1, :slots] for r in range(n_row)], axis=1)
    oh_d[...] = (
        (every == lax.broadcasted_iota(jnp.int32, (col_blocks, n_row * slots), 0))
        .astype(f32)
        .astype(bf16)
    )
    every = jnp.concatenate([cidx[c][1:2, :slots] for c in range(n_col)], axis=1)
    oh_p[...] = (
        (every == lax.broadcasted_iota(jnp.int32, (row_blocks, n_col * slots), 0))
        .astype(f32)
        .astype(bf16)
    )
    for c in kcopies:
        c.wait()

    which = lax.broadcasted_iota(jnp.int32, (GROUP, block), 0)

    def spread(pieces, g):
        lhs = pieces[GROUP * g : GROUP * (g + 1), :]
        return [jnp.where(which == s, lhs, 0.0).astype(bf16) for s in range(GROUP)]

    def exchange_start(buf, ssem, rsem, par, me, axis, peers, ch):
        part = pl.ds(ch * per_chunk, per_chunk)
        src = buf.at[par, me, part, :]
        for p in peers:
            remote(src, src, ssem.at[par, p, ch], rsem.at[par, me, ch], axis, p).start()

    def exchange_wait(buf, ssem, rsem, par, axis, peers):
        for ch in range(CHUNKS):
            part = pl.ds(ch * per_chunk, per_chunk)
            for p in peers:
                dst = buf.at[par, p, part, :]
                remote(dst, dst, ssem.at[par, p, ch], rsem.at[par, p, ch], axis, p).wait()

    def tile_start(buf, ssem, rsem, par, me, axis, peers):
        src = buf.at[par, me]
        for p in peers:
            remote(src, src, ssem.at[par, p], rsem.at[par, me], axis, p).start()

    def tile_wait(buf, ssem, rsem, par, axis, peers):
        for p in peers:
            dst = buf.at[par, p]
            remote(dst, dst, ssem.at[par, p], rsem.at[par, p], axis, p).wait()

    def total(buf, par, n):
        acc = buf[par, 0]
        for i in range(1, n):
            acc = acc + buf[par, i]
        acc = jnp.sum(acc, axis=0, keepdims=True)
        return jnp.sum(acc, axis=1, keepdims=True)

    def body(k, carry):
        omega, taken = carry
        par = lax.rem(k, 2)
        old = lax.rem(k + 1, 2)
        flag_now = jnp.where(k <= ITERS - 3, restart_ref[k], 0) == 1
        flag_old = (
            jnp.where((k >= 1) & (k <= ITERS - 2), restart_ref[jnp.maximum(k - 1, 0)], 0) == 1
        )

        tile_start(dyr, ys_sem, yr_sem, par, me_r, "row", row_peers)
        y_low = y_s[...].astype(bf16)
        pieces = jnp.dot(oh_r[...], y_low, preferred_element_type=f32)
        for g in range(groups):
            lhs = jnp.concatenate(spread(pieces, g), axis=1)
            prod = jnp.dot(
                lhs,
                k_v[pl.ds(g * GROUP * block, GROUP * block), :],
                preferred_element_type=f32,
            )
            drecv[par, me_r, pl.ds(g * GROUP, GROUP), :] = prod.astype(bf16)
            if (g + 1) * GROUP % per_chunk == 0:
                exchange_start(
                    drecv, ds_sem, dr_sem, par, me_r, "row", row_peers,
                    (g + 1) * GROUP // per_chunk - 1,
                )
        tile_wait(dyr, ys_sem, yr_sem, par, "row", row_peers)
        drift_x = total(dxr, old, n_col) / total_cols + epsilon
        drift_y = total(dyr, par, n_row) / total_rows + epsilon
        omega_next = jnp.sqrt(omega) * jnp.sqrt(jnp.sqrt(drift_x / drift_y))
        omega = jnp.where(flag_old, omega_next, omega)
        tau = step_scale / omega
        sigma = step_scale * omega

        exchange_wait(drecv, ds_sem, dr_sem, par, "row", row_peers)
        dual = jnp.dot(
            oh_d[...],
            drecv[par].reshape(n_row * slots, block),
            preferred_element_type=f32,
        )
        x = x_s[...]
        x_next = jnp.minimum(jnp.maximum(x - tau * (obj_s[...] - dual), 0.0), ub_s[...])
        extrap = (2.0 * x_next - x).astype(bf16)
        pieces = jnp.dot(oh_c[...], extrap, preferred_element_type=f32)

        taken = taken + 1.0
        inv = 1.0 / taken
        sum_x = sx_s[...] + x_next
        mean_x = sum_x * inv
        gap = mean_x - ax_s[...]
        dxr[par, me_c] = fold(gap * gap)
        tile_start(dxr, xs_sem, xr_sem, par, me_c, "col", col_peers)
        x_s[...] = jnp.where(flag_now, mean_x, x_next)
        ax_s[...] = jnp.where(flag_now, mean_x, ax_s[...])
        sx_s[...] = jnp.where(flag_now, 0.0, sum_x)

        for g in range(groups):
            prod = None
            for s, lhs in enumerate(spread(pieces, g)):
                term = lax.dot_general(
                    lhs,
                    k_v[pl.ds((g * GROUP + s) * block, block), :],
                    (((1,), (1,)), ((), ())),
                    preferred_element_type=f32,
                )
                prod = term if prod is None else prod + term
            precv[par, me_c, pl.ds(g * GROUP, GROUP), :] = prod.astype(bf16)
            if (g + 1) * GROUP % per_chunk == 0:
                exchange_start(
                    precv, ps_sem, pr_sem, par, me_c, "col", col_peers,
                    (g + 1) * GROUP // per_chunk - 1,
                )
        tile_wait(dxr, xs_sem, xr_sem, par, "col", col_peers)
        exchange_wait(precv, ps_sem, pr_sem, par, "col", col_peers)
        primal = jnp.dot(
            oh_p[...],
            precv[par].reshape(n_col * slots, block),
            preferred_element_type=f32,
        )
        y_next = jnp.maximum(y_s[...] + sigma * (dem_s[...] - primal), 0.0)
        sum_y = sy_s[...] + y_next
        mean_y = sum_y * inv
        gap = mean_y - ay_s[...]
        dyr[old, me_r] = fold(gap * gap)
        y_s[...] = jnp.where(flag_now, mean_y, y_next)
        ay_s[...] = jnp.where(flag_now, mean_y, ay_s[...])
        sy_s[...] = jnp.where(flag_now, 0.0, sum_y)
        taken = jnp.where(flag_now, 0.0, taken)
        return omega, taken

    one = jnp.ones((1, 1), f32)
    lax.fori_loop(0, ITERS, body, (one, jnp.zeros((1, 1), f32)))
    xo_ref[pl.ds(0, col_blocks, stride=2), :] = x_s[:, :half]
    xo_ref[pl.ds(1, col_blocks, stride=2), :] = x_s[:, half:]
    yo_ref[pl.ds(0, row_blocks, stride=2), :] = y_s[:, :half]
    yo_ref[pl.ds(1, row_blocks, stride=2), :] = y_s[:, half:]


def shards(
    block_values,
    block_rows,
    block_cols,
    live_count,
    objective,
    upper_bound,
    demand,
    primal_start,
    dual_start,
    restart_at,
):
    slots, block = block_values.shape[2], block_values.shape[3]
    n_row = lax.axis_size("row")
    n_col = lax.axis_size("col")
    row_blocks = demand.shape[0] // block
    col_blocks = objective.shape[0] // block
    live = jnp.arange(slots, dtype=jnp.int32) < live_count[0, 0]
    index = jnp.stack([block_cols[0, 0], block_rows[0, 0]])
    index = jnp.where(live[None, :], index, -1)
    index = jnp.pad(index, ((0, 6), (0, 128 - slots)), constant_values=-1)
    wide = lambda v: v.reshape(-1, 128)
    f32, bf16 = jnp.float32, jnp.bfloat16
    vmem = pl.BlockSpec(memory_space=pltpu.VMEM)
    dma = pltpu.SemaphoreType.DMA
    x_shape, y_shape = (col_blocks, block), (row_blocks, block)
    x_out, y_out = pl.pallas_call(
        functools.partial(kernel, n_row, n_col, slots, block),
        out_shape=(
            jax.ShapeDtypeStruct((col_blocks * block // 128, 128), f32),
            jax.ShapeDtypeStruct((row_blocks * block // 128, 128), f32),
        ),
        in_specs=[
            pl.BlockSpec(memory_space=pl.ANY),
            vmem,
            pl.BlockSpec(memory_space=pltpu.SMEM),
            vmem,
            vmem,
            vmem,
            vmem,
            vmem,
        ],
        out_specs=(vmem, vmem),
        scratch_shapes=[
            pltpu.VMEM((slots * block, block), bf16),
            pltpu.VMEM((n_row, 8, 128), jnp.int32),
            pltpu.VMEM((n_col, 8, 128), jnp.int32),
            pltpu.VMEM((col_blocks, n_row * slots), bf16),
            pltpu.VMEM((row_blocks, n_col * slots), bf16),
            pltpu.VMEM((slots, col_blocks), bf16),
            pltpu.VMEM((slots, row_blocks), bf16),
            pltpu.VMEM((2, n_row, slots, block), bf16),
            pltpu.VMEM((2, n_col, slots, block), bf16),
            pltpu.VMEM((2, n_row, 8, 128), f32),
            pltpu.VMEM((2, n_col, 8, 128), f32),
            pltpu.VMEM(x_shape, f32),
            pltpu.VMEM(x_shape, f32),
            pltpu.VMEM(y_shape, f32),
            pltpu.VMEM(x_shape, f32),
            pltpu.VMEM(y_shape, f32),
            pltpu.VMEM(x_shape, f32),
            pltpu.VMEM(y_shape, f32),
            pltpu.VMEM(x_shape, f32),
            pltpu.VMEM(y_shape, f32),
            dma((slots // GROUP,)),
            dma((n_row,)),
            dma((n_row,)),
            dma((n_col,)),
            dma((n_col,)),
            dma((2, n_row, CHUNKS)),
            dma((2, n_row, CHUNKS)),
            dma((2, n_col, CHUNKS)),
            dma((2, n_col, CHUNKS)),
            dma((2, n_row)),
            dma((2, n_row)),
            dma((2, n_col)),
            dma((2, n_col)),
        ],
        compiler_params=pltpu.CompilerParams(collective_id=0, has_side_effects=True),
    )(
        block_values.reshape(slots * block, block),
        index,
        restart_at,
        wide(objective),
        wide(upper_bound),
        wide(demand),
        wide(primal_start),
        wide(dual_start),
    )
    return x_out.reshape(-1), y_out.reshape(-1)


def solution(mesh):
    placed = (
        P("row", "col", None, None, None),
        P("row", "col", None),
        P("row", "col", None),
        P("row", "col"),
        P("col"),
        P("col"),
        P("row"),
        P("col"),
        P("row"),
        P(),
    )
    return jax.shard_map(
        shards, mesh=mesh, in_specs=placed, out_specs=(P("col"), P("row")), check_vma=False
    )
```

time: 850 us -> 115 us (0.14)
  waiting for transfers between devices: 440 us -> 0 us
  blocking collectives: 242 us -> 0 us
  Pallas kernels: 0 us -> 109 us
  matrix products: 87.5 us -> 0 us
  between operations: 27.6 us -> 1.29 us
  other arithmetic: 25.7 us -> 0.69 us
  local copies, waits for them, and re-layouts: 24.5 us -> 3.74 us
    psum x16 -> x0, waiting for transfers between devices: 440 us -> none  [the longest x8 268 us: shards(): lax.psum(jnp.einsum('tr,ti->ri', row_onehot, products, precision=lax.Prec...]
    psum x6 -> x0, blocking collectives: 242 us -> none  [shards(): square_x = lax.psum(jnp.sum(gap_x * gap_x), ('row', 'col'))]
    pallas_call x0 -> x1, Pallas kernels: none -> 109 us  [shards(): pl.pallas_call(functools.partial(kernel, n_row, n_col, slots, block), out...]
    dot_general x32 -> x0, matrix products: 87.5 us -> none  [the longest x8 45.1 us: shards(): jnp.einsum('tij,tj->ti', slot_values, pieces, preferred_element_type=jnp....]
    gather x16 -> x0, local copies, waits for them, and re-layouts: 11.2 us -> none  [the longest x8 5.6 us: shards(): pieces = extrap_low.reshape(col_blocks, block_size)[cols_index]]
    convert_element_type x16 -> x0, other arithmetic: 9.15 us -> none  [the longest x8 5.19 us: shards(): y_low = y.astype(jnp.bfloat16)]
    unnamed x32 -> x2, local copies, waits for them, and re-layouts: 12.1 us -> 3.14 us
  transfers between devices with their start and end apart: 16 -> 0, of which waited for: 16 -> 0; matrix products, arithmetic and copies ran while one was open for 1% -> 0% of each run, Pallas kernels for 0% -> 0%
where the time goes in v1:
time: 115 us
  Pallas kernels  109 us (95%)
  local copies, waits for them, and re-layouts  3.74 us (3%)
  between operations  1.29 us (1%)
    pallas_call x1, Pallas kernels, shards(): pl.pallas_call(functools.partial(kernel, n_row, n_col, slots, block), out...  109 us
    unnamed x2, local copies, waits for them, and re-layouts  3.14 us

profile of v1, /device:TPU:0, one launch (start us, length us, event | category | flops | bytes accessed | tf_op | source)
XLA Modules:
  0.0 114.7 jit_solution(8385738075025837981)
XLA Ops:
  1.3 0.7 add_select_fusion
  2.0 0.6 pad.4.idx_ref
  2.6 109.0 %shard_map.113 = (f32[512,128]{1,0:T(8,128)}, f32[128,128]{1,0:T(8,128)}) custom-call(bf16[16384,256]{1,0:T(8,128)(2,1)} %bitcast.12, s32[8,128]{1,0:T(8,128)} %pad.4.idx_ref, s32[8]{0:T(128)} %restart_ref.1, f32[512,128]{1,0:T(8,128)} %bitcast.13, f32[512,128]{1,0:T(8,128)} %bitcast.14, f32[128,128]{1,0:T(8,128)} %bitcast.17, f32[512,128]{1,0:T(8,128)} %bitcast.15, ...), custom_call_target="tpu_custom_call" | custom-call | tf_op jit(solution)/shard_map/pallas_call | solution.py:332
  111.6 1.7 %copy.15 = f32[65536]{0:T(1024)} copy(f32[65536]{0:T(1024)} %bitcast.16) | data formatting | bytes 524288
  113.2 1.5 %copy.16 = f32[16384]{0:T(1024)} copy(f32[16384]{0:T(1024)} %bitcast.19) | data formatting | bytes 131072
  (1 shorter events, 0.0 us)

commit v2 on v1

v2 whole, which is shorter than its diff:
```python
import functools

import jax
import jax.numpy as jnp
from jax import lax
from jax.experimental import pallas as pl
from jax.experimental.pallas import tpu as pltpu
from jax.sharding import PartitionSpec as P

ITERS = 8
GROUP = 16
SPLIT = 2

step_scale = 0.3
epsilon = 1e-06

MESH = pl.DeviceIdType.MESH


def fold(v):
    rows, lanes = v.shape
    v = jnp.sum(v.reshape(rows // 8, 8, lanes), axis=0)
    out = v[:, 0:128]
    for i in range(1, lanes // 128):
        out = out + v[:, 128 * i : 128 * (i + 1)]
    return out


def peers_of(me, n):
    if n & (n - 1):
        return [lax.rem(me + d, n) for d in range(n - 1, 0, -1)]
    out = []
    for m in sorted(range(1, n), key=lambda m: (-(m // 2).bit_count(), m)):
        p = me
        bit = 1
        while bit < n:
            if m & bit:
                p = p + bit - 2 * bit * lax.rem(lax.div(me, bit), 2)
            bit *= 2
        out.append(p)
    return out


def kernel(
    n_row,
    n_col,
    slots,
    block,
    k_hbm,
    cols_ref,
    rows_ref,
    live_ref,
    restart_ref,
    obj_hbm,
    ub_hbm,
    dem_hbm,
    x0_hbm,
    y0_hbm,
    xo_hbm,
    yo_hbm,
    k_v,
    kt_v,
    idx,
    ridx,
    cidx,
    oh_d,
    oh_p,
    oh_c,
    oh_r,
    drecv,
    precv,
    dyr,
    dxr,
    raw_x,
    raw_y,
    obj_s,
    ub_s,
    dem_s,
    x_s,
    y_s,
    ax_s,
    ay_s,
    sx_s,
    sy_s,
    ksem,
    rawsem,
    outsem,
    is_r,
    ir_r,
    is_c,
    ir_c,
    ds_sem,
    dr_sem,
    ps_sem,
    pr_sem,
    ys_sem,
    yr_sem,
    xs_sem,
    xr_sem,
):
    me_r = lax.axis_index("row")
    me_c = lax.axis_index("col")
    col_blocks = x_s.shape[0]
    row_blocks = y_s.shape[0]
    total_cols = float(col_blocks * block * n_col)
    total_rows = float(row_blocks * block * n_row)
    bf16, f32 = jnp.bfloat16, jnp.float32
    groups = slots // GROUP
    half = block // 2
    chunks = ((0, SPLIT * GROUP), (SPLIT * GROUP, slots - SPLIT * GROUP))

    row_peers = peers_of(me_r, n_row)
    col_peers = peers_of(me_c, n_col)
    barrier = pltpu.get_barrier_semaphore()
    for p in row_peers:
        pl.semaphore_signal(barrier, inc=1, device_id={"row": p}, device_id_type=MESH)
    for p in col_peers:
        pl.semaphore_signal(barrier, inc=1, device_id={"col": p}, device_id_type=MESH)

    y_in = pltpu.make_async_copy(y0_hbm, raw_y.at[0], rawsem.at[0])
    y_in.start()
    kcopies = []
    for g in range(groups):
        part = pl.ds(g * GROUP * block, GROUP * block)
        c = pltpu.make_async_copy(k_hbm.at[part, :], k_v.at[part, :], ksem.at[g])
        c.start()
        kcopies.append(c)
    ins = [
        pltpu.make_async_copy(dem_hbm, raw_y.at[1], rawsem.at[1]),
        pltpu.make_async_copy(x0_hbm, raw_x.at[0], rawsem.at[2]),
        pltpu.make_async_copy(obj_hbm, raw_x.at[1], rawsem.at[3]),
        pltpu.make_async_copy(ub_hbm, raw_x.at[2], rawsem.at[4]),
    ]
    for c in ins:
        c.start()
    out_x = pltpu.make_async_copy(raw_x.at[0], xo_hbm, outsem.at[0])
    out_y = pltpu.make_async_copy(raw_y.at[0], yo_hbm, outsem.at[1])

    def widen(ref, at, n):
        return jnp.concatenate(
            [ref[at, pl.ds(0, n, stride=2), :], ref[at, pl.ds(1, n, stride=2), :]], axis=1
        )

    def narrow(ref, value, n):
        ref[0, pl.ds(0, n, stride=2), :] = value[:, :half]
        ref[0, pl.ds(1, n, stride=2), :] = value[:, half:]

    live = lax.broadcasted_iota(jnp.int32, (1, slots), 1) < live_ref[0, 0]
    idx[...] = jnp.full((8, 128), -1, jnp.int32)
    idx[0:1, :slots] = jnp.where(live, cols_ref[...], -1)
    idx[1:2, :slots] = jnp.where(live, rows_ref[...], -1)
    own = idx[...]
    oh = (own[0:1, :] == lax.broadcasted_iota(jnp.int32, (col_blocks, 128), 0)).astype(f32)
    oh_c[...] = jnp.transpose(oh)[:slots, :].astype(bf16)
    pad = -(-row_blocks // 128) * 128
    oh = (own[1:2, :] == lax.broadcasted_iota(jnp.int32, (pad, 128), 0)).astype(f32)
    oh_r[...] = jnp.transpose(oh)[:slots, :row_blocks].astype(bf16)
    ridx[me_r] = own
    cidx[me_c] = own
    dyr[0, me_r] = jnp.zeros((8, 128), f32)
    dyr[1, me_r] = jnp.zeros((8, 128), f32)
    for c in range(n_col):
        dxr[1, c] = jnp.zeros((8, 128), f32)

    y_in.wait()
    y_first = widen(raw_y, 0, row_blocks)
    y_s[...] = y_first
    ay_s[...] = y_first
    sy_s[...] = jnp.zeros_like(y_first)

    pl.semaphore_wait(barrier, n_row + n_col - 2)

    def remote(src, dst, ssem, rsem, axis, peer):
        return pltpu.make_async_remote_copy(
            src_ref=src,
            dst_ref=dst,
            send_sem=ssem,
            recv_sem=rsem,
            device_id={axis: peer},
            device_id_type=MESH,
        )

    for p in row_peers:
        remote(idx, ridx.at[me_r], is_r.at[p], ir_r.at[me_r], "row", p).start()
    for p in col_peers:
        remote(idx, cidx.at[me_c], is_c.at[p], ir_c.at[me_c], "col", p).start()

    def settle():
        for c in ins:
            c.wait()
        dem_s[...] = widen(raw_y, 1, row_blocks)
        obj_s[...] = widen(raw_x, 1, col_blocks)
        ub_s[...] = widen(raw_x, 2, col_blocks)
        x_first = widen(raw_x, 0, col_blocks)
        x_s[...] = x_first
        ax_s[...] = x_first
        sx_s[...] = jnp.zeros_like(x_first)

        def turn(t, carry):
            for u in range(4):
                part = pl.ds(pl.multiple_of((t * 4 + u) * block, block), block)
                kt_v[part, :] = jnp.transpose(k_v[part, :])
            return carry

        lax.fori_loop(0, slots // 4, turn, 0)
        for p in row_peers:
            remote(idx, ridx.at[p], is_r.at[p], ir_r.at[p], "row", p).wait()
        for p in col_peers:
            remote(idx, cidx.at[p], is_c.at[p], ir_c.at[p], "col", p).wait()
        every = jnp.concatenate([ridx[r][0:1, :slots] for r in range(n_row)], axis=1)
        oh_d[...] = (
            (every == lax.broadcasted_iota(jnp.int32, (col_blocks, n_row * slots), 0))
            .astype(f32)
            .astype(bf16)
        )
        every = jnp.concatenate([cidx[c][1:2, :slots] for c in range(n_col)], axis=1)
        oh_p[...] = (
            (every == lax.broadcasted_iota(jnp.int32, (row_blocks, n_col * slots), 0))
            .astype(f32)
            .astype(bf16)
        )

    which = lax.broadcasted_iota(jnp.int32, (GROUP, block), 0)

    def exchange(buf, ssem, rsem, par, me, axis, peers, ch, act):
        part = pl.ds(*chunks[ch])
        if act == "start":
            src = buf.at[par, me, part, :]
            for p in peers:
                remote(src, src, ssem.at[par, p, ch], rsem.at[par, me, ch], axis, p).start()
            return
        for p in peers:
            dst = buf.at[par, p, part, :]
            c = remote(dst, dst, ssem.at[par, p, ch], rsem.at[par, p, ch], axis, p)
            c.wait_recv() if act == "recv" else c.wait_send()

    def tile(buf, ssem, rsem, par, me, axis, peers, act):
        if act == "start":
            src = buf.at[par, me]
            for p in peers:
                remote(src, src, ssem.at[par, p], rsem.at[par, me], axis, p).start()
            return
        for p in peers:
            dst = buf.at[par, p]
            remote(dst, dst, ssem.at[par, p], rsem.at[par, p], axis, p).wait()

    def both(*args):
        exchange(*args[:-1], 0, args[-1])
        exchange(*args[:-1], 1, args[-1])

    def products(pieces, mat, buf, me, par, args, first):
        for g in range(groups):
            if first:
                kcopies[g].wait()
            part = pieces[GROUP * g : GROUP * (g + 1), :]
            lhs = jnp.concatenate(
                [jnp.where(which == s, part, 0.0).astype(bf16) for s in range(GROUP)], axis=1
            )
            prod = jnp.dot(
                lhs,
                mat[pl.ds(g * GROUP * block, GROUP * block), :],
                preferred_element_type=f32,
            )
            buf[par, me, pl.ds(g * GROUP, GROUP), :] = prod.astype(bf16)
            if g + 1 == SPLIT:
                exchange(*args, 0, "start")
        exchange(*args, 1, "start")

    def total(buf, par, n):
        acc = buf[par, 0]
        for i in range(1, n):
            acc = acc + buf[par, i]
        acc = jnp.sum(acc, axis=0, keepdims=True)
        return jnp.sum(acc, axis=1, keepdims=True)

    def body(k, carry, first=False):
        omega, taken = carry
        par = lax.rem(k, 2)
        old = lax.rem(k + 1, 2)
        d_args = (drecv, ds_sem, dr_sem, par, me_r, "row", row_peers)
        p_args = (precv, ps_sem, pr_sem, par, me_c, "col", col_peers)
        flag_now = jnp.where(k <= ITERS - 3, restart_ref[k], 0) == 1

        if not first:
            tile(dyr, ys_sem, yr_sem, par, me_r, "row", row_peers, "start")
        y_low = y_s[...].astype(bf16)
        pieces = jnp.dot(oh_r[...], y_low, preferred_element_type=f32)
        products(pieces, k_v, drecv, me_r, par, d_args, first)
        if first:
            settle()
        else:
            both(precv, ps_sem, pr_sem, old, me_c, "col", col_peers, "sent")
            flag_old = jnp.where(k <= ITERS - 2, restart_ref[k - 1], 0) == 1
            tile(dyr, ys_sem, yr_sem, par, me_r, "row", row_peers, "wait")
            drift_x = total(dxr, old, n_col) / total_cols + epsilon
            drift_y = total(dyr, par, n_row) / total_rows + epsilon
            omega_next = jnp.sqrt(omega) * jnp.sqrt(jnp.sqrt(drift_x / drift_y))
            omega = jnp.where(flag_old, omega_next, omega)
        tau = step_scale / omega
        sigma = step_scale * omega

        both(*d_args, "recv")
        dual = jnp.dot(
            oh_d[...],
            drecv[par].reshape(n_row * slots, block),
            preferred_element_type=f32,
        )
        x = x_s[...]
        x_next = jnp.minimum(jnp.maximum(x - tau * (obj_s[...] - dual), 0.0), ub_s[...])
        extrap = (2.0 * x_next - x).astype(bf16)
        pieces = jnp.dot(oh_c[...], extrap, preferred_element_type=f32)
        x_s[...] = x_next
        products(pieces, kt_v, precv, me_c, par, p_args, False)

        x_next = x_s[...]
        taken = taken + 1.0
        inv = 1.0 / taken
        sum_x = sx_s[...] + x_next
        mean_x = sum_x * inv
        gap = mean_x - ax_s[...]
        dxr[par, me_c] = fold(gap * gap)
        tile(dxr, xs_sem, xr_sem, par, me_c, "col", col_peers, "start")
        x_last = jnp.where(flag_now, mean_x, x_next)
        x_s[...] = x_last
        ax_s[...] = jnp.where(flag_now, mean_x, ax_s[...])
        sx_s[...] = jnp.where(flag_now, 0.0, sum_x)
        both(*d_args, "sent")
        if not first:

            @pl.when(k == ITERS - 1)
            def _():
                narrow(raw_x, x_s[...], col_blocks)
                out_x.start()

        both(*p_args, "recv")
        primal = jnp.dot(
            oh_p[...],
            precv[par].reshape(n_col * slots, block),
            preferred_element_type=f32,
        )
        y_next = jnp.maximum(y_s[...] + sigma * (dem_s[...] - primal), 0.0)
        sum_y = sy_s[...] + y_next
        mean_y = sum_y * inv
        gap = mean_y - ay_s[...]
        dyr[old, me_r] = fold(gap * gap)
        y_s[...] = jnp.where(flag_now, mean_y, y_next)
        ay_s[...] = jnp.where(flag_now, mean_y, ay_s[...])
        sy_s[...] = jnp.where(flag_now, 0.0, sum_y)
        taken = jnp.where(flag_now, 0.0, taken)
        tile(dxr, xs_sem, xr_sem, par, me_c, "col", col_peers, "wait")
        return omega, taken

    carry = body(0, (jnp.ones((1, 1), f32), jnp.zeros((1, 1), f32)), True)
    lax.fori_loop(1, ITERS, body, carry)
    narrow(raw_y, y_s[...], row_blocks)
    out_y.start()
    both(precv, ps_sem, pr_sem, (ITERS - 1) % 2, me_c, "col", col_peers, "sent")
    out_x.wait()
    out_y.wait()


def shards(
    block_values,
    block_rows,
    block_cols,
    live_count,
    objective,
    upper_bound,
    demand,
    primal_start,
    dual_start,
    restart_at,
):
    slots, block = block_values.shape[2], block_values.shape[3]
    n_row = lax.axis_size("row")
    n_col = lax.axis_size("col")
    row_blocks = demand.shape[0] // block
    col_blocks = objective.shape[0] // block
    wide = lambda v: v.reshape(-1, 128)
    f32, bf16 = jnp.float32, jnp.bfloat16
    vmem = pl.BlockSpec(memory_space=pltpu.VMEM)
    smem = pl.BlockSpec(memory_space=pltpu.SMEM)
    hbm = pl.BlockSpec(memory_space=pl.ANY)
    dma = pltpu.SemaphoreType.DMA
    x_shape, y_shape = (col_blocks, block), (row_blocks, block)
    x_out, y_out = pl.pallas_call(
        functools.partial(kernel, n_row, n_col, slots, block),
        out_shape=(
            jax.ShapeDtypeStruct((col_blocks * block // 128, 128), f32),
            jax.ShapeDtypeStruct((row_blocks * block // 128, 128), f32),
        ),
        in_specs=[
            hbm,
            vmem,
            vmem,
            smem,
            smem,
            hbm,
            hbm,
            hbm,
            hbm,
            hbm,
        ],
        out_specs=(hbm, hbm),
        scratch_shapes=[
            pltpu.VMEM((slots * block, block), bf16),
            pltpu.VMEM((slots * block, block), bf16),
            pltpu.VMEM((8, 128), jnp.int32),
            pltpu.VMEM((n_row, 8, 128), jnp.int32),
            pltpu.VMEM((n_col, 8, 128), jnp.int32),
            pltpu.VMEM((col_blocks, n_row * slots), bf16),
            pltpu.VMEM((row_blocks, n_col * slots), bf16),
            pltpu.VMEM((slots, col_blocks), bf16),
            pltpu.VMEM((slots, row_blocks), bf16),
            pltpu.VMEM((2, n_row, slots, block), bf16),
            pltpu.VMEM((2, n_col, slots, block), bf16),
            pltpu.VMEM((2, n_row, 8, 128), f32),
            pltpu.VMEM((2, n_col, 8, 128), f32),
            pltpu.VMEM((3, col_blocks * block // 128, 128), f32),
            pltpu.VMEM((2, row_blocks * block // 128, 128), f32),
            pltpu.VMEM(x_shape, f32),
            pltpu.VMEM(x_shape, f32),
            pltpu.VMEM(y_shape, f32),
            pltpu.VMEM(x_shape, f32),
            pltpu.VMEM(y_shape, f32),
            pltpu.VMEM(x_shape, f32),
            pltpu.VMEM(y_shape, f32),
            pltpu.VMEM(x_shape, f32),
            pltpu.VMEM(y_shape, f32),
            dma((slots // GROUP,)),
            dma((5,)),
            dma((2,)),
            dma((n_row,)),
            dma((n_row,)),
            dma((n_col,)),
            dma((n_col,)),
            dma((2, n_row, 2)),
            dma((2, n_row, 2)),
            dma((2, n_col, 2)),
            dma((2, n_col, 2)),
            dma((2, n_row)),
            dma((2, n_row)),
            dma((2, n_col)),
            dma((2, n_col)),
        ],
        compiler_params=pltpu.CompilerParams(collective_id=0, has_side_effects=True),
    )(
        block_values.reshape(slots * block, block),
        block_cols[0],
        block_rows[0],
        live_count,
        restart_at,
        wide(objective),
        wide(upper_bound),
        wide(demand),
        wide(primal_start),
        wide(dual_start),
    )
    return x_out.reshape(-1), y_out.reshape(-1)


def solution(mesh):
    placed = (
        P("row", "col", None, None, None),
        P("row", "col", None),
        P("row", "col", None),
        P("row", "col"),
        P("col"),
        P("col"),
        P("row"),
        P("col"),
        P("row"),
        P(),
    )
    return jax.shard_map(
        shards, mesh=mesh, in_specs=placed, out_specs=(P("col"), P("row")), check_vma=False
    )
```

time: 115 us -> 108 us (0.939)
  Pallas kernels: 109 us -> 103 us
    pallas_call x1, Pallas kernels: 109 us -> 103 us  [shards(): pl.pallas_call(functools.partial(kernel, n_row, n_col, slots, block), out...]
where the time goes in v2:
time: 108 us
  Pallas kernels  103 us (95%)
  local copies, waits for them, and re-layouts  3.14 us (3%)
  between operations  1.29 us (1%)
    pallas_call x1, Pallas kernels, shards(): pl.pallas_call(functools.partial(kernel, n_row, n_col, slots, block), out...  103 us
    unnamed x2, local copies, waits for them, and re-layouts  3.14 us

profile of v2, /device:TPU:0, one launch (start us, length us, event | category | flops | bytes accessed | tf_op | source)
XLA Modules:
  0.0 107.6 jit_solution(1798088705659336802)
XLA Ops:
  1.3 103.2 %shard_map.113 = (f32[512,128]{1,0:T(8,128)}, f32[128,128]{1,0:T(8,128)}) custom-call(bf16[16384,256]{1,0:T(8,128)(2,1)} %bitcast.10, s32[1,64]{1,0:T(1,128)} %bitcast.18, s32[1,64]{1,0:T(1,128)} %bitcast.19, s32[1,1]{1,0:T(1,128)S(6)} %copy.14.live_ref, s32[8]{0:T(128)} %restart_ref.1, f32[512,128]{1,0:T(8,128)} %bitcast.11, f32[512,128]{1,0:T(8,128)} %bitcast.12, ...), custom_call_target="tpu_custom_call" | custom-call | tf_op jit(solution)/shard_map/pallas_call | solution.py:386
  104.5 1.7 %copy.15 = f32[65536]{0:T(1024)} copy(f32[65536]{0:T(1024)} %bitcast.14) | data formatting | bytes 524288
  106.2 1.5 %copy.16 = f32[16384]{0:T(1024)} copy(f32[16384]{0:T(1024)} %bitcast.17) | data formatting | bytes 131072

commit v3 on v2

--- a/solution.py
+++ b/solution.py
@@ -9,7 +9,6 @@
 
 ITERS = 8
 GROUP = 16
-SPLIT = 2
 
 step_scale = 0.3
 epsilon = 1e-06
@@ -23,7 +22,7 @@
     out = v[:, 0:128]
     for i in range(1, lanes // 128):
         out = out + v[:, 128 * i : 128 * (i + 1)]
-    return out
+    return jnp.sum(out, axis=0, keepdims=True)
 
 
 def peers_of(me, n):
@@ -107,7 +106,8 @@
     bf16, f32 = jnp.bfloat16, jnp.float32
     groups = slots // GROUP
     half = block // 2
-    chunks = ((0, SPLIT * GROUP), (SPLIT * GROUP, slots - SPLIT * GROUP))
+    split = groups // 2
+    part_slots = slots // 2
 
     row_peers = peers_of(me_r, n_row)
     col_peers = peers_of(me_c, n_col)
@@ -157,10 +157,10 @@
     oh_r[...] = jnp.transpose(oh)[:slots, :row_blocks].astype(bf16)
     ridx[me_r] = own
     cidx[me_c] = own
-    dyr[0, me_r] = jnp.zeros((8, 128), f32)
-    dyr[1, me_r] = jnp.zeros((8, 128), f32)
+    dyr[0, me_r] = jnp.zeros((1, 128), f32)
+    dyr[1, me_r] = jnp.zeros((1, 128), f32)
     for c in range(n_col):
-        dxr[1, c] = jnp.zeros((8, 128), f32)
+        dxr[1, c] = jnp.zeros((1, 128), f32)
 
     y_in.wait()
     y_first = widen(raw_y, 0, row_blocks)
@@ -207,30 +207,25 @@
             remote(idx, ridx.at[p], is_r.at[p], ir_r.at[p], "row", p).wait()
         for p in col_peers:
             remote(idx, cidx.at[p], is_c.at[p], ir_c.at[p], "col", p).wait()
-        every = jnp.concatenate([ridx[r][0:1, :slots] for r in range(n_row)], axis=1)
-        oh_d[...] = (
-            (every == lax.broadcasted_iota(jnp.int32, (col_blocks, n_row * slots), 0))
-            .astype(f32)
-            .astype(bf16)
-        )
-        every = jnp.concatenate([cidx[c][1:2, :slots] for c in range(n_col)], axis=1)
-        oh_p[...] = (
-            (every == lax.broadcasted_iota(jnp.int32, (row_blocks, n_col * slots), 0))
-            .astype(f32)
-            .astype(bf16)
-        )
+        for ch in range(2):
+            lanes = slice(ch * part_slots, (ch + 1) * part_slots)
+            every = jnp.concatenate([ridx[r][0:1, lanes] for r in range(n_row)], axis=1)
+            at = lax.broadcasted_iota(jnp.int32, (col_blocks, n_row * part_slots), 0)
+            oh_d[ch] = (every == at).astype(f32).astype(bf16)
+            every = jnp.concatenate([cidx[c][1:2, lanes] for c in range(n_col)], axis=1)
+            at = lax.broadcasted_iota(jnp.int32, (row_blocks, n_col * part_slots), 0)
+            oh_p[ch] = (every == at).astype(f32).astype(bf16)
 
     which = lax.broadcasted_iota(jnp.int32, (GROUP, block), 0)
 
     def exchange(buf, ssem, rsem, par, me, axis, peers, ch, act):
-        part = pl.ds(*chunks[ch])
         if act == "start":
-            src = buf.at[par, me, part, :]
+            src = buf.at[par, ch, me]
             for p in peers:
                 remote(src, src, ssem.at[par, p, ch], rsem.at[par, me, ch], axis, p).start()
             return
         for p in peers:
-            dst = buf.at[par, p, part, :]
+            dst = buf.at[par, ch, p]
             c = remote(dst, dst, ssem.at[par, p, ch], rsem.at[par, p, ch], axis, p)
             c.wait_recv() if act == "recv" else c.wait_send()
 
@@ -261,10 +256,22 @@
                 mat[pl.ds(g * GROUP * block, GROUP * block), :],
                 preferred_element_type=f32,
             )
-            buf[par, me, pl.ds(g * GROUP, GROUP), :] = prod.astype(bf16)
-            if g + 1 == SPLIT:
+            buf[par, g // split, me, pl.ds(g % split * GROUP, GROUP), :] = prod.astype(bf16)
+            if g + 1 == split:
                 exchange(*args, 0, "start")
         exchange(*args, 1, "start")
+
+    def gather_sum(oh, args, n):
+        acc = None
+        for ch in range(2):
+            exchange(*args, ch, "recv")
+            term = jnp.dot(
+                oh[ch],
+                args[0][args[3], ch].reshape(n * part_slots, block),
+                preferred_element_type=f32,
+            )
+            acc = term if acc is None else acc + term
+        return acc
 
     def total(buf, par, n):
         acc = buf[par, 0]
@@ -299,12 +306,7 @@
         tau = step_scale / omega
         sigma = step_scale * omega
 
-        both(*d_args, "recv")
-        dual = jnp.dot(
-            oh_d[...],
-            drecv[par].reshape(n_row * slots, block),
-            preferred_element_type=f32,
-        )
+        dual = gather_sum(oh_d, d_args, n_row)
         x = x_s[...]
         x_next = jnp.minimum(jnp.maximum(x - tau * (obj_s[...] - dual), 0.0), ub_s[...])
         extrap = (2.0 * x_next - x).astype(bf16)
@@ -332,12 +334,7 @@
                 narrow(raw_x, x_s[...], col_blocks)
                 out_x.start()
 
-        both(*p_args, "recv")
-        primal = jnp.dot(
-            oh_p[...],
-            precv[par].reshape(n_col * slots, block),
-            preferred_element_type=f32,
-        )
+        primal = gather_sum(oh_p, p_args, n_col)
         y_next = jnp.maximum(y_s[...] + sigma * (dem_s[...] - primal), 0.0)
         sum_y = sy_s[...] + y_next
         mean_y = sum_y * inv
@@ -408,14 +405,14 @@
             pltpu.VMEM((8, 128), jnp.int32),
             pltpu.VMEM((n_row, 8, 128), jnp.int32),
             pltpu.VMEM((n_col, 8, 128), jnp.int32),
-            pltpu.VMEM((col_blocks, n_row * slots), bf16),
-            pltpu.VMEM((row_blocks, n_col * slots), bf16),
+            pltpu.VMEM((2, col_blocks, n_row * slots // 2), bf16),
+            pltpu.VMEM((2, row_blocks, n_col * slots // 2), bf16),
             pltpu.VMEM((slots, col_blocks), bf16),
             pltpu.VMEM((slots, row_blocks), bf16),
-            pltpu.VMEM((2, n_row, slots, block), bf16),
-            pltpu.VMEM((2, n_col, slots, block), bf16),
-            pltpu.VMEM((2, n_row, 8, 128), f32),
-            pltpu.VMEM((2, n_col, 8, 128), f32),
+            pltpu.VMEM((2, 2, n_row, slots // 2, block), bf16),
+            pltpu.VMEM((2, 2, n_col, slots // 2, block), bf16),
+            pltpu.VMEM((2, n_row, 1, 128), f32),
+            pltpu.VMEM((2, n_col, 1, 128), f32),
             pltpu.VMEM((3, col_blocks * block // 128, 128), f32),
             pltpu.VMEM((2, row_blocks * block // 128, 128), f32),
             pltpu.VMEM(x_shape, f32),

time: 108 us -> 106 us (0.981)
    pallas_call x1, Pallas kernels: 103 us -> 102 us  [shards(): pl.pallas_call(functools.partial(kernel, n_row, n_col, slots, block), out...]
where the time goes in v3:
time: 106 us
  Pallas kernels  102 us (96%)
  local copies, waits for them, and re-layouts  3.14 us (3%)
  between operations  1.29 us (1%)
    pallas_call x1, Pallas kernels, shards(): pl.pallas_call(functools.partial(kernel, n_row, n_col, slots, block), out...  102 us
    unnamed x2, local copies, waits for them, and re-layouts  3.14 us

profile of v3, /device:TPU:0, one launch (start us, length us, event | category | flops | bytes accessed | tf_op | source)
XLA Modules:
  0.0 106.0 jit_solution(13598493783650871076)
XLA Ops:
  1.3 101.6 %shard_map.113 = (f32[512,128]{1,0:T(8,128)}, f32[128,128]{1,0:T(8,128)}) custom-call(bf16[16384,256]{1,0:T(8,128)(2,1)} %bitcast.10, s32[1,64]{1,0:T(1,128)} %bitcast.18, s32[1,64]{1,0:T(1,128)} %bitcast.19, s32[1,1]{1,0:T(1,128)S(6)} %copy.14.live_ref, s32[8]{0:T(128)} %restart_ref.1, f32[512,128]{1,0:T(8,128)} %bitcast.11, f32[512,128]{1,0:T(8,128)} %bitcast.12, ...), custom_call_target="tpu_custom_call" | custom-call | tf_op jit(solution)/shard_map/pallas_call | solution.py:383
  102.9 1.7 %copy.15 = f32[65536]{0:T(1024)} copy(f32[65536]{0:T(1024)} %bitcast.14) | data formatting | bytes 524288
  104.6 1.5 %copy.16 = f32[16384]{0:T(1024)} copy(f32[16384]{0:T(1024)} %bitcast.17) | data formatting | bytes 131072
